TPU v7x, 512 devices: a whole 4x8x8 slice. The times are simulated.
512 devices in a mesh: seq: 128 (over y, z, core), head: 4 (over x).
Axes of the slice: x: 4, y: 8, z: 8, core: 2. Of those that a mesh axis runs over, the one named last changes fastest.
Arguments:
- tokens: bfloat16 [16384, 2048], P('seq', 'head'), as said below
- w_query: bfloat16 [2048, 1024], P(None, 'head'), may hold values from -0.125 to 0.125
- w_key: bfloat16 [2048, 1024], P(None, 'head')
- w_value: bfloat16 [2048, 1024], P(None, 'head'), may hold values from -0.125 to 0.125
- gate_codes: int32 [16384, 8], P('seq', 'head'), may hold values from 28 to 1572854, as said below
- beta_codes: int32 [16384, 8], P('seq', 'head'), may hold values from 32 to 256
- norm_gain: float32 [128], replicated, may hold values from 0.25 to 1.75
- w_out: bfloat16 [1024, 2048], P('head'), may hold values from -0.1875 to 0.1875
Outputs:
- mixed: bfloat16 [16384, 2048], P('seq', 'head')
Inputs may be any that keep to these rules, and one draw needn't show every extreme that they name: `gate_codes`: codes are positive; the sweep's gates are those of one recording, identical law in every draw. `tokens`: activations of order one to ten.
All inputs are finite; a program needn't handle non-finite values.
Results may differ from a plain program's by a relative error of at most 0.0049.
Values may be sent and summed in bfloat16 or wider, within the bound.
A program may use at most 128 MiB of HBM per device.

v0:
```python
import jax
import jax.numpy as jnp
from jax import lax
from jax.sharding import PartitionSpec as P

SPAN = 64


def entering(part, axis, combine, identity):
    place = lax.axis_index(axis)
    gathered = jax.tree.map(lambda a: lax.all_gather(a, axis), part)
    state = jax.tree.map(lambda a, e: jnp.zeros_like(a) + jnp.asarray(e, a.dtype), part, identity)

    def one(step, state):
        return combine(
            state, jax.tree.map(lambda a: lax.dynamic_index_in_dim(a, step, 0, False), gathered)
        )

    return lax.fori_loop(0, place, one, state)


def shards(tokens, w_query, w_key, w_value, gate_codes, beta_codes, norm_gain, w_out):
    highest = lax.Precision.HIGHEST
    tok_rows = tokens.shape[0]
    heads_here = gate_codes.shape[1]
    head_size = norm_gain.shape[0]
    n_spans = tok_rows // SPAN
    piece = lax.all_gather(tokens, "head", axis=1, tiled=True)
    query, key_rows, value = tuple(
        (
            jnp.dot(piece, weight, preferred_element_type=jnp.float32)
            for weight in (w_query, w_key, w_value)
        )
    )

    def split_heads(array):
        return array.reshape(n_spans, SPAN, heads_here, head_size).transpose(2, 0, 1, 3)

    queries = split_heads(query)
    unit_keys = split_heads(key_rows)
    unit_keys = unit_keys * lax.rsqrt(jnp.sum(unit_keys * unit_keys, -1, keepdims=True) + 1e-06)
    values = split_heads(value)
    decay_log = (
        (-gate_codes.astype(jnp.float32) / 2097152.0)
        .reshape(n_spans, SPAN, heads_here)
        .transpose(2, 0, 1)
    )
    log_decay = jnp.cumsum(decay_log, axis=-1)
    betas = (
        (beta_codes.astype(jnp.float32) / 256.0)
        .reshape(n_spans, SPAN, heads_here)
        .transpose(2, 0, 1)
    )
    positions = jnp.arange(SPAN)
    lower_incl = positions[:, None] >= positions[None, :]
    lower_strict = positions[:, None] > positions[None, :]
    gaps = log_decay[..., :, None] - log_decay[..., None, :]
    inclusive = jnp.where(lower_incl, jnp.exp(jnp.where(lower_incl, gaps, 0.0)), 0.0)
    strict = jnp.where(lower_strict, inclusive, 0.0)
    key_dots = jnp.einsum("hctd,hcid->hcti", unit_keys, unit_keys, precision=highest)
    system = jnp.eye(SPAN, dtype=jnp.float32) + betas[..., :, None] * key_dots * strict
    right = jnp.concatenate(
        [betas[..., None] * unit_keys * jnp.exp(log_decay)[..., None], betas[..., None] * values],
        axis=-1,
    )
    solved = jax.scipy.linalg.solve_triangular(system, right, lower=True, unit_diagonal=True)
    wy_keys = solved[..., :head_size]
    wy_values = solved[..., head_size:]
    query_dots = jnp.einsum("hctd,hcid->hcti", queries, unit_keys, precision=highest) * inclusive
    intra = jnp.einsum("hcti,hciv->hctv", query_dots, wy_values, precision=highest)
    query_eff = queries * jnp.exp(log_decay)[..., None] - jnp.einsum(
        "hcti,hcik->hctk", query_dots, wy_keys, precision=highest
    )
    last_log = log_decay[..., -1]
    key_tail = unit_keys * jnp.exp(last_log[..., None] - log_decay)[..., None]
    identity_mat = jnp.eye(head_size, dtype=jnp.float32)
    span_maps = jnp.exp(last_log)[..., None, None] * identity_mat - jnp.einsum(
        "hctk,hctj->hckj", wy_keys, key_tail, precision=highest
    )
    span_adds = jnp.einsum("hctv,hctk->hcvk", wy_values, key_tail, precision=highest)
    span_maps = jnp.moveaxis(span_maps, 1, 0)
    span_adds = jnp.moveaxis(span_adds, 1, 0)
    zero_state = jnp.zeros((heads_here, head_size, head_size), jnp.float32)
    unit_maps = jnp.broadcast_to(identity_mat, (heads_here, head_size, head_size))

    def advance(carry, inputs):
        state, product = carry
        step_map, step_add = inputs
        new_state = jnp.einsum("hvk,hkj->hvj", state, step_map, precision=highest) + step_add
        new_product = jnp.einsum("hik,hkj->hij", product, step_map, precision=highest)
        return ((new_state, new_product), (state, product))

    def summarize(carry, inputs):
        new_carry, _ = advance(carry, inputs)
        return (new_carry, None)

    def combine(earlier, later):
        return (
            jnp.einsum("hik,hkj->hij", earlier[0], later[0], precision=highest),
            jnp.einsum("hvk,hkj->hvj", earlier[1], later[0], precision=highest) + later[1],
        )

    (summary_state, summary_map), _ = lax.scan(
        summarize, (zero_state, unit_maps), (span_maps, span_adds)
    )
    _, incoming = entering((summary_map, summary_state), "seq", combine, (unit_maps, zero_state))

    def replay(state, inputs):
        step_map, step_add = inputs
        return (jnp.einsum("hvk,hkj->hvj", state, step_map, precision=highest) + step_add, state)

    _, starts = lax.scan(replay, incoming, (span_maps, span_adds))
    outputs = intra + jnp.einsum("hctk,chvk->hctv", query_eff, starts, precision=highest)
    normed = outputs * lax.rsqrt(jnp.mean(outputs * outputs, -1, keepdims=True) + 1e-06) * norm_gain
    normed = (
        normed.astype(jnp.bfloat16).transpose(1, 2, 0, 3).reshape(tok_rows, heads_here * head_size)
    )
    partial_out = jnp.dot(normed, w_out, preferred_element_type=jnp.float32)
    return lax.psum_scatter(partial_out, "head", scatter_dimension=1, tiled=True).astype(
        jnp.bfloat16
    )


def solution(mesh):
    return jax.shard_map(
        shards,
        mesh=mesh,
        in_specs=(
            P("seq", "head"),
            P(None, "head"),
            P(None, "head"),
            P(None, "head"),
            P("seq", "head"),
            P("seq", "head"),
            P(),
            P("head", None),
        ),
        out_specs=P("seq", "head"),
        check_vma=False,
    )
```

profile of v0, /device:TPU:8, one launch (start us, length us, event | category | flops | bytes accessed | tf_op | source)
XLA Modules:
  0.0 591.1 jit_solution(8923890875720144227)
XLA Ops:
  8.2 13.3 %all_gather.15 = bf16[128,2048]{1,0:T(8,128)(2,1)S(1)} all-gather(bf16[128,512]{1,0:T(8,128)(2,1)} %param.14), channel_id=1, replica_groups=mesh['seq'=128,'head'=4] {'head'}, dimensions={1}, use_global_device_ids=true | all-gather | bytes 655360 | tf_op jit(solution)/shard_map/all_gather | solution.py:28
  21.5 1.5 fusion.56
  24.0 1.5 fusion.57
  26.2 19.7 %custom-call.4 = f32[2,2,1,64,64]{3,4,2,1,0:T(8,128)S(1)} custom-call(f32[2,2,1,64,64]{4,3,2,1,0:T(8,128)S(1)} %fusion.24), custom_call_target="InvertDiagBlocksLowerTriangular" | custom-call | tf_op jit(solution)/shard_map/jit(_solve_triangular)/vmap(vmap())/triangular_solve | solution.py:66
  48.2 1.2 while.39
  51.1 1.5 fusion.55
  53.7 101.4 %all-gather.5.cloned.1.call-done = f32[256,128,128]{2,1,0:T(8,128)} async-done(((f32[2,128,128]{2,1,0:T(8,128)}), f32[256,128,128]{2,1,0:T(8,128)}) %all-gather.5.cloned.1.call-update) | async-done | bytes 16777232 | tf_op jit(solution)/shard_map/all_gather | solution.py:11
  155.1 101.3 %all-gather.7.cloned.1.call-done = f32[256,128,128]{2,1,0:T(8,128)} async-done(((f32[2,128,128]{2,1,0:T(8,128)}), f32[256,128,128]{2,1,0:T(8,128)}) %all-gather.7.cloned.1.call-update) | async-done | bytes 16777232 | tf_op jit(solution)/shard_map/all_gather | solution.py:11
  256.4 37.9 %while.37 = (s32[]{:T(128)}, f32[2,128,128]{1,2,0:T(8,128)S(1)}, s32[]{:T(128)}, f32[128,2,128,128]{3,2,1,0:T(8,128)}, f32[128,2,128,128]{3,2,1,0:T(8,128)}, /*index=5*/s32[]{:T(128)}, s32[]{:T(128)}, s32[]{:T(128)}) while((s32[]{:T(128)}, f32[2,128,128]{1,2,0:T(8,128)S(1)}, s32[]{:T(128)}, f32[128,2,128,128]{3,2,1,0:T(8,128)}, ...), condition=%wide.region_5.6_spmd, body=%wide.region_4.5_spmd.sunk | while | flops 50364420 | bytes 1310855 | solution.py:19
  256.5 0.9 constant_dynamic-slice_fusion.2
  257.5 1.3 fusion.85
  258.8 0.9 constant_dynamic-slice_fusion.2
  259.9 1.3 fusion.85
  261.2 0.9 constant_dynamic-slice_fusion.2
  262.2 1.3 fusion.85
  264.6 1.3 fusion.85
  267.0 1.3 fusion.85
  269.3 1.3 fusion.85
  271.7 1.3 fusion.85
  274.1 1.3 fusion.85
  276.4 1.3 fusion.85
  278.8 1.3 fusion.85
  281.2 1.3 fusion.85
  283.5 1.3 fusion.85
  285.9 1.3 fusion.85
  287.3 0.9 constant_dynamic-slice_fusion.2
  288.3 1.3 fusion.85
  290.7 1.3 fusion.85
  293.0 1.3 fusion.85
  295.7 1.3 fusion.42
  297.0 286.0 %reduce-scatter.2.cloned.1.call-done = f32[128,512]{1,0:T(8,128)} async-done(((f32[128,2048]{1,0:T(8,128)}), f32[128,512]{1,0:T(8,128)}) %reduce-scatter.2.cloned.1.call-update) | async-done | bytes 262160 | tf_op jit(solution)/shard_map/reduce_scatter | solution.py:119
  582.9 1.6 convert_element_type.34
  (108 shorter events, 23.8 us)
Async XLA Ops:
  6.5 289.1 %copy-start = (bf16[256,2048]{1,0:T(8,128)(2,1)S(1)}, bf16[256,2048]{1,0:T(8,128)(2,1)}, u32[]{:S(2)}) copy-start(bf16[256,2048]{1,0:T(8,128)(2,1)} %param.21) | copy-start | bytes 3145732
  6.5 148.5 %all-gather.5.cloned.1.call-start = ((), (), s32[]{:S(2)}) async-start(), calls=%async_computation.2 | async-start | bytes 16908288 | tf_op jit(solution)/shard_map/all_gather | solution.py:11
  7.5 288.0 %copy-start.1 = (f32[128]{0:T(128)S(1)}, f32[128]{0:T(128)}, u32[]{:S(2)}) copy-start(f32[128]{0:T(128)} %param.20) | copy-start | bytes 1540
  50.2 206.2 %all-gather.7.cloned.1.call-start = ((), (), s32[]{:S(2)}) async-start(), calls=%async_computation.3 | async-start | bytes 16908288 | tf_op jit(solution)/shard_map/all_gather | solution.py:11
  51.1 531.9 %reduce-scatter.2.cloned.1.call-start = ((), (), s32[]{:S(2)}) async-start(), calls=%async_computation.1 | async-start | bytes 1310720 | tf_op jit(solution)/shard_map/reduce_scatter | solution.py:119
Sparse Core Ops, SparseCore 0:
  50.4 104.6 all-gather.4
  158.2 98.1 all-gather.6
  297.1 285.7 reduce-scatter.1
where the time goes:
time: 596 us; the launch traced here: 591 us
  waiting for transfers between devices  489 us (82%)
  matrix products  31.8 us (5%)
  other arithmetic  23.8 us (4%)
  local copies, waits for them, and re-layouts  19 us (3%)
  between operations  13.4 us (2%)
  blocking collectives  13.3 us (2%)
    reduce_scatter x1, waiting for transfers between devices, shards(): lax.psum_scatter(partial_out, 'head', scatter_dimension=1, tiled=True)  286 us
    all_gather x2, waiting for transfers between devices, entering(): gathered = jax.tree.map(lambda a: lax.all_gather(a, axis), part)  203 us
    dot_general x16, matrix products, combine(): jnp.einsum('hvk,hkj->hvj', earlier[1], later[0], precision=highest)  20.7 us
    another operation x3, other arithmetic, shards(): jax.scipy.linalg.solve_triangular(system, right, lower=True, unit_diagona...  19.7 us
    dynamic_slice x32, local copies, waits for them, and re-layouts, one(): lax.dynamic_index_in_dim(a, step, 0, False)  16.2 us
    all_gather x1, blocking collectives, shards(): piece = lax.all_gather(tokens, 'head', axis=1, tiled=True)  13.3 us
  transfers between devices with their start and end apart: 3, of which 3 were waited for; matrix products, arithmetic and copies ran while one was open for 1% of the time, Pallas kernels for 0%

commit v1 on v0

--- a/solution.py
+++ b/solution.py
@@ -4,6 +4,11 @@
 from jax.sharding import PartitionSpec as P
 
 SPAN = 64
+
+
+def lift_the_view(matrix, a_name):
+    vec_out = jnp.stack(lax.psum(1, a_name) * [matrix], axis=0)
+    return jnp.concatenate(lax.all_to_all(vec_out, a_name, 0, 0), axis=1)
 
 
 def entering(part, axis, combine, identity):
@@ -25,7 +30,7 @@
     heads_here = gate_codes.shape[1]
     head_size = norm_gain.shape[0]
     n_spans = tok_rows // SPAN
-    piece = lax.all_gather(tokens, "head", axis=1, tiled=True)
+    piece = lift_the_view(tokens, "head")
     query, key_rows, value = tuple(
         (
             jnp.dot(piece, weight, preferred_element_type=jnp.float32)

time: 596 us -> 600 us (level)
  blocking collectives: 13.3 us -> 0 us
  local copies, waits for them, and re-layouts: 19 us -> 30.9 us
    all_gather x1 -> x0, blocking collectives: 13.3 us -> none  [shards(): piece = lax.all_gather(tokens, 'head', axis=1, tiled=True)]
    dot_general x0 -> x4, local copies, waits for them, and re-layouts: none -> 6.65 us  [shards(): jnp.dot(piece, weight, preferred_element_type=jnp.float32)]
  transfers between devices with their start and end apart: 3 -> 4, of which waited for: 3 -> 4; matrix products, arithmetic and copies ran while one was open for 1% -> 2% of each run, Pallas kernels for 0% -> 0%
where the time goes in v1:
time: 600 us; the launch traced here: 595 us
  waiting for transfers between devices  488 us (81%)
  matrix products  32.8 us (5%)
  local copies, waits for them, and re-layouts  30.9 us (5%)
  other arithmetic  25 us (4%)
  between operations  13.4 us (2%)
    reduce_scatter x1, waiting for transfers between devices, shards(): lax.psum_scatter(partial_out, 'head', scatter_dimension=1, tiled=True)  286 us
    all_gather x2, waiting for transfers between devices, entering(): gathered = jax.tree.map(lambda a: lax.all_gather(a, axis), part)  200 us
    dot_general x16, matrix products, combine(): jnp.einsum('hvk,hkj->hvj', earlier[1], later[0], precision=highest)  20.7 us
    another operation x3, other arithmetic, shards(): jax.scipy.linalg.solve_triangular(system, right, lower=True, unit_diagona...  19.7 us
    dynamic_slice x32, local copies, waits for them, and re-layouts, one(): lax.dynamic_index_in_dim(a, step, 0, False)  16.2 us
  transfers between devices with their start and end apart: 4, of which 4 were waited for; matrix products, arithmetic and copies ran while one was open for 2% of the time, Pallas kernels for 0%

profile of v1, /device:TPU:8, one launch (start us, length us, event | category | flops | bytes accessed | tf_op | source)
XLA Modules:
  0.0 595.4 jit_solution(337850250392734940)
XLA Ops:
  6.5 1.8 stack.2
  8.4 4.3 all-to-all-start
  15.7 2.3 copy.137
  17.9 1.5 copy.138
  20.1 2.1 all-to-all-done
  23.4 1.4 reshape.85
  24.8 1.8 multiply_reduce_fusion.1
  27.1 19.7 %custom-call.4 = f32[2,2,1,64,64]{3,4,2,1,0:T(8,128)S(1)} custom-call(f32[2,2,1,64,64]{4,3,2,1,0:T(8,128)S(1)} %fusion.25), custom_call_target="InvertDiagBlocksLowerTriangular" | custom-call | tf_op jit(solution)/shard_map/jit(_solve_triangular)/vmap(vmap())/triangular_solve | solution.py:71
  54.2 1.5 copy.136
  58.0 98.7 %all-gather.5.cloned.1.call-done = f32[256,128,128]{2,1,0:T(8,128)} async-done(((f32[2,128,128]{2,1,0:T(8,128)}), f32[256,128,128]{2,1,0:T(8,128)}) %all-gather.5.cloned.1.call-update) | async-done | bytes 16777232 | tf_op jit(solution)/shard_map/all_gather | solution.py:16
  156.7 101.3 %all-gather.7.cloned.1.call-done = f32[256,128,128]{2,1,0:T(8,128)} async-done(((f32[2,128,128]{2,1,0:T(8,128)}), f32[256,128,128]{2,1,0:T(8,128)}) %all-gather.7.cloned.1.call-update) | async-done | bytes 16777232 | tf_op jit(solution)/shard_map/all_gather | solution.py:16
  258.0 37.9 %while.37 = (s32[]{:T(128)}, f32[2,128,128]{1,2,0:T(8,128)S(1)}, s32[]{:T(128)}, f32[128,2,128,128]{3,2,1,0:T(8,128)}, f32[128,2,128,128]{3,2,1,0:T(8,128)}, /*index=5*/s32[]{:T(128)}, s32[]{:T(128)}, s32[]{:T(128)}) while((s32[]{:T(128)}, f32[2,128,128]{1,2,0:T(8,128)S(1)}, s32[]{:T(128)}, f32[128,2,128,128]{3,2,1,0:T(8,128)}, ...), condition=%wide.region_5.6_spmd, body=%wide.region_4.5_spmd.sunk | while | flops 50364420 | bytes 1310855 | solution.py:24
  259.1 1.3 fusion.79
  261.4 1.3 fusion.79
  263.8 1.3 fusion.79
  266.2 1.3 fusion.79
  268.5 1.3 fusion.79
  270.9 1.3 fusion.79
  273.3 1.3 fusion.79
  275.6 1.3 fusion.79
  278.0 1.3 fusion.79
  280.4 1.3 fusion.79
  282.7 1.3 fusion.79
  285.1 1.3 fusion.79
  287.5 1.3 fusion.79
  289.9 1.3 fusion.79
  292.2 1.3 fusion.79
  294.6 1.3 fusion.79
  295.9 1.9 while.38
  297.8 1.4 multiply_reduce_fusion
  301.4 285.8 %reduce-scatter.2.cloned.1.call-done = f32[128,512]{1,0:T(8,128)} async-done(((f32[128,2048]{1,0:T(8,128)}), f32[128,512]{1,0:T(8,128)}) %reduce-scatter.2.cloned.1.call-update) | async-done | bytes 262160 | tf_op jit(solution)/shard_map/reduce_scatter | solution.py:124
  587.2 1.6 convert_element_type.34
  (116 shorter events, 36.4 us)
Async XLA Ops:
  6.5 293.6 %copy-start = (bf16[256,2048]{1,0:T(8,128)(2,1)S(1)}, bf16[256,2048]{1,0:T(8,128)(2,1)}, u32[]{:S(2)}) copy-start(bf16[256,2048]{1,0:T(8,128)(2,1)} %param.21) | copy-start | bytes 3145732
  8.4 13.8 %all-to-all-start = ((bf16[4,128,512]{2,1,0:T(8,128)(2,1)}), bf16[4,128,512]{2,1,0:T(8,128)(2,1)S(1)}, u32[]{:S(2)}, u32[]{:S(2)}) async-start(bf16[4,128,512]{2,1,0:T(8,128)(2,1)} %stack.2), calls=%async_computation | async-start | bytes 1048576 | tf_op jit(solution)/shard_map/all_to_all | solution.py:11
  12.7 144.0 %all-gather.5.cloned.1.call-start = ((), (), s32[]{:S(2)}) async-start(), calls=%async_computation.3 | async-start | bytes 16908288 | tf_op jit(solution)/shard_map/all_gather | solution.py:16
  26.7 23.0 %copy-start.1 = (f32[2,2,64,128]{3,2,0,1:T(8,128)}, f32[2,2,64,128]{3,2,0,1:T(8,128)S(1)}, u32[]{:S(2)}) copy-start(f32[2,2,64,128]{3,2,0,1:T(8,128)S(1)} %get-tuple-element.207) | copy-start | bytes 393220
  53.3 204.6 %all-gather.7.cloned.1.call-start = ((), (), s32[]{:S(2)}) async-start(), calls=%async_computation.4 | async-start | bytes 16908288 | tf_op jit(solution)/shard_map/all_gather | solution.py:16
  54.1 533.1 %reduce-scatter.2.cloned.1.call-start = ((), (), s32[]{:S(2)}) async-start(), calls=%async_computation.2 | async-start | bytes 1310720 | tf_op jit(solution)/shard_map/reduce_scatter | solution.py:124
Sparse Core Ops, SparseCore 0:
  53.5 103.1 all-gather.4
  159.8 98.1 all-gather.6
  301.5 285.6 reduce-scatter.1
